TPU v7x, 32 devices: a whole 2x2x4 slice. The times are simulated.
32 devices in a mesh: dp: 4 (over z), ctx: 2 (over core), tp: 4 (over y, x).
Axes of the slice: x: 2, y: 2, z: 4, core: 2. Of those that a mesh axis runs over, the one named last changes fastest.
Arguments:
- block_in: bfloat16 [8192, 2048], P(('dp', 'ctx')), may hold values from -6 to 6
- query_proj: bfloat16 [2048, 2048], P('dp', 'tp'), may hold values from -0.125 to 0.125
- forget_proj: bfloat16 [2048, 2048], P('dp', 'tp'), may hold values from -0.0625 to 0.0625
- value_proj: bfloat16 [2048, 2048], P('dp', 'tp'), may hold values from -0.125 to 0.125
- outgate_proj: bfloat16 [2048, 2048], P('dp', 'tp'), may hold values from -0.125 to 0.125
- out_proj: bfloat16 [2048, 2048], P('tp', 'dp'), may hold values from -0.125 to 0.125
- ffn_gate: bfloat16 [2048, 5632], P('dp', 'tp'), may hold values from -0.125 to 0.125
- ffn_up: bfloat16 [2048, 5632], P('dp', 'tp'), may hold values from -0.125 to 0.125
- ffn_down: bfloat16 [5632, 2048], P('tp', 'dp'), may hold values from -0.078125 to 0.078125
- first_gain: float32 [2048], replicated, may hold values from 0.5 to 1.5
- second_gain: float32 [2048], replicated, may hold values from 0.5 to 1.5
- group_gain: float32 [2048], P('tp'), may hold values from 0.5 to 1.5
- forget_bias: float32 [2048], P('tp'), may hold values from 3 to 12
- bound_table: float32 [24, 2048], P(None, 'tp'), may hold values from -4 to 4
- layer_index: int32 [1], replicated, may hold values from 1 to 23
- second_start: int32 [4], P('dp'), may hold values from 1 to 2048, as said below
- cotangent: bfloat16 [8192, 2048], P(('dp', 'ctx')), may hold values from -6 to 6
Outputs:
- block_out: bfloat16 [8192, 2048], P(('dp', 'ctx'))
- input_grad: float32 [8192, 2048], P(('dp', 'ctx'))
- query_grad: float32 [2048, 2048], P('dp', 'tp')
- forget_grad: float32 [2048, 2048], P('dp', 'tp')
- value_grad: float32 [2048, 2048], P('dp', 'tp')
- outgate_grad: float32 [2048, 2048], P('dp', 'tp')
- out_proj_grad: float32 [2048, 2048], P('tp', 'dp')
- ffn_gate_grad: float32 [2048, 5632], P('dp', 'tp')
- ffn_up_grad: float32 [2048, 5632], P('dp', 'tp')
- ffn_down_grad: float32 [5632, 2048], P('tp', 'dp')
- first_gain_grad: float32 [2048], replicated
- second_gain_grad: float32 [2048], replicated
- group_gain_grad: float32 [2048], P('tp')
- forget_bias_grad: float32 [2048], P('tp')
- bound_table_grad: float32 [24, 2048], P(None, 'tp')
Inputs may be any that keep to these rules, and one draw needn't show every extreme that they name: second_start[p] is 2048 where pack p is one whole sequence, and otherwise the position inside the pack where its second sequence begins; pack 0 is always one whole sequence and pack 1 always holds two. layer_index names a row of bound_table other than the first.
All inputs are finite; a program needn't handle non-finite values.
Results may differ from a plain program's by a relative error of at most 0.018.
Values may be sent and summed in bfloat16 or wider, within the bound.
No kernel may reach another device: no remote copies, remote signals or barrier semaphores. Data moves between devices by JAX's collectives and lax.ppermute only.
A program may use at most 384 MiB of HBM per device.

v0:
```python
import jax
import jax.numpy as jnp
from jax import lax
from jax.sharding import PartitionSpec as P

HEAD = 128
BLOCK = 32
HIGH = lax.Precision.HIGHEST
EPS_NORM = 1e-06
EPS_GROUP = 1e-05


def carried_in(value, axis, join, neutral):
    count, mine = (lax.axis_size(axis), lax.axis_index(axis))
    pieces = jax.tree.map(lambda part: lax.all_gather(part, axis), value)
    total = jax.tree.map(
        lambda part, zero: jnp.full_like(part, 0) + jnp.asarray(zero, part.dtype), value, neutral
    )

    def hop(position, total):
        longer = join(total, jax.tree.map(lambda part: part[position], pieces))
        return jax.tree.map(lambda new, old: jnp.where(position < mine, new, old), longer, total)

    return lax.fori_loop(0, count - 1, hop, total)


def carried_in_2(array, axis, combine, identity):
    peers, index = (lax.axis_size(axis), lax.axis_index(axis))
    everything = jax.tree.map(
        lambda part, kind: lax.all_gather(part.astype(kind), axis),
        array,
        jax.tree.map(lambda a: jnp.bfloat16 if a.dtype == jnp.float32 else a.dtype, array),
    )
    start = jax.tree.map(
        lambda part, zero: jnp.broadcast_to(jnp.asarray(zero, part.dtype), part.shape),
        array,
        identity,
    )

    def hop(k, before):
        at = peers - 1 - k
        reached = at > index
        new = combine(
            before, jax.tree.map(lambda part, own: part[at].astype(own.dtype), everything, array)
        )
        return jax.tree.map(lambda a, b: jnp.where(reached, a, b), new, before)

    return lax.fori_loop(0, peers, hop, start)


def rms_norm(rows_in, gain_vec):
    return (
        rows_in
        * lax.rsqrt(jnp.mean(rows_in * rows_in, axis=-1, keepdims=True) + EPS_NORM)
        * gain_vec
    )


def head_norm(mixed, pre_gate, gain_vec, head_count):
    row_count = mixed.shape[0]
    grouped = mixed.reshape(row_count, head_count, -1)
    scaled = grouped * lax.rsqrt(jnp.mean(grouped * grouped, axis=-1, keepdims=True) + EPS_GROUP)
    return scaled.reshape(row_count, -1) * gain_vec * jax.nn.silu(pre_gate)


def lower_bound(bound_rows, which_layer):
    weights = jax.nn.softmax(bound_rows, axis=0)
    rising = jnp.cumsum(weights, axis=0) - weights[0:1]
    picked = (
        lax.broadcasted_iota(jnp.int32, (bound_rows.shape[0], 1), 0) == which_layer[0]
    ).astype(bound_rows.dtype)
    return jnp.sum(rising * picked, axis=0)


def gate_values(pre_query, pre_forget, bias_vec, bound_vec):
    shifted = pre_forget + bias_vec
    forget = bound_vec + (1.0 - bound_vec) * jax.nn.sigmoid(shifted)
    return (jax.nn.silu(pre_query), (1.0 - bound_vec) * jax.nn.sigmoid(-shifted), jnp.log(forget))


def chain_link(earlier, later):
    return (earlier[0] * later[0], later[0][..., None] * earlier[1] + later[1])


def contract_last(left_side, right_side):
    return lax.dot_general(
        left_side, right_side, (((1,), (1,)), ((), ())), preferred_element_type=jnp.float32
    )


def contract_first(left_side, right_side):
    return lax.dot_general(
        left_side, right_side, (((0,), (0,)), ((), ())), preferred_element_type=jnp.float32
    )


def block_parts(queries, key_rows, values, log_forget, doc_ids, prev_doc, block_len):
    length, head_count, feature = queries.shape
    block_count = length // block_len
    blocked = (block_count, block_len, head_count, feature)
    queries = queries.reshape(blocked)
    key_rows = key_rows.reshape(blocked)
    values = values.reshape(blocked)
    decays = jnp.cumsum(log_forget.reshape(blocked), axis=1)
    doc_ids = doc_ids.reshape(block_count, block_len)
    before = jnp.concatenate([jnp.reshape(prev_doc, (1,)), doc_ids[:-1, block_len - 1]])
    middle = decays[:, block_len // 2 : block_len // 2 + 1]
    final_decay = decays[:, block_len - 1 :]
    scores = jnp.einsum(
        "nthc,nshc->nhts",
        queries * jnp.exp(decays - middle),
        key_rows * jnp.exp(middle - decays),
        precision=HIGH,
    )
    causal = lax.broadcasted_iota(jnp.int32, (block_len, block_len), 0) >= lax.broadcasted_iota(
        jnp.int32, (block_len, block_len), 1
    )
    allowed = causal[None] & (doc_ids[:, :, None] == doc_ids[:, None, :])
    scores = jnp.where(allowed[:, None], scores, 0.0)
    inside = jnp.einsum("nhts,nshe->nthe", scores, values, precision=HIGH)
    in_tail = (doc_ids == doc_ids[:, block_len - 1 :]).astype(decays.dtype)
    ending = key_rows * jnp.exp(final_decay - decays) * in_tail[:, :, None, None]
    states = jnp.einsum("nshc,nshe->nhce", ending, values, precision=HIGH)
    kept_flag = (doc_ids[:, block_len - 1] == before).astype(decays.dtype)
    carried = jnp.exp(final_decay[:, 0]) * kept_flag[:, None, None]
    entering = (doc_ids == before[:, None]).astype(decays.dtype)
    reached = queries * jnp.exp(decays) * entering[:, :, None, None]
    prefix_decay, prefix_state = lax.associative_scan(chain_link, (carried, states), axis=0)
    return (inside, reached, prefix_decay, prefix_state)


def finish(pieces, state_in):
    inside, reached, prefix_decay, prefix_state = pieces
    state_ends = prefix_decay[..., None] * state_in[None] + prefix_state
    state_starts = jnp.concatenate([state_in[None], state_ends[:-1]], axis=0)
    outside = jnp.einsum("nthc,nhce->nthe", reached, state_starts, precision=HIGH)
    summed = inside + outside
    block_count, block_len, head_count, feature = summed.shape
    return (summed.reshape(block_count * block_len, head_count, feature), state_ends[-1])


def body(
    block_in,
    query_proj,
    forget_proj,
    value_proj,
    outgate_proj,
    out_proj,
    ffn_gate,
    ffn_up,
    ffn_down,
    first_gain,
    second_gain,
    group_gain,
    forget_bias,
    bound_table,
    layer_index,
    second_start,
    cotangent,
):
    row_count = block_in.shape[0]
    local_width = query_proj.shape[1]
    head_count = local_width // HEAD
    hidden_width = ffn_gate.shape[1]
    inputs = block_in.astype(jnp.float32)
    first_low = rms_norm(inputs, first_gain).astype(jnp.bfloat16)
    mix_local = jnp.concatenate([query_proj, forget_proj, value_proj, outgate_proj], axis=1)
    ffn_local = jnp.concatenate([ffn_gate, ffn_up], axis=1)
    mix_full, out_full = (
        lax.all_gather(mix_local, "dp", axis=0, tiled=True),
        lax.all_gather(out_proj, "dp", axis=1, tiled=True),
    )
    projected = jnp.dot(first_low, mix_full, preferred_element_type=jnp.float32)
    pre_query = projected[:, :local_width]
    pre_forget = projected[:, local_width : 2 * local_width]
    pre_value = projected[:, 2 * local_width : 3 * local_width]
    pre_outgate = projected[:, 3 * local_width :]
    bound_vec = lower_bound(bound_table, layer_index)
    queries, key_rows, log_forget = gate_values(pre_query, pre_forget, forget_bias, bound_vec)
    offset = lax.axis_index("ctx") * row_count
    doc_ids = (offset + lax.iota(jnp.int32, row_count) >= second_start[0]).astype(jnp.int32)
    prev_doc = (offset - 1 >= second_start[0]).astype(jnp.int32)

    def to_heads(flat):
        return flat.reshape(row_count, head_count, HEAD)

    def mixer(queries_in, keys_in, values_in, logs_in, state_in):
        return finish(
            block_parts(queries_in, keys_in, values_in, logs_in, doc_ids, prev_doc, BLOCK), state_in
        )

    pieces = block_parts(
        to_heads(queries),
        to_heads(key_rows),
        to_heads(pre_value),
        to_heads(log_forget),
        doc_ids,
        prev_doc,
        BLOCK,
    )
    identity = (
        jnp.ones((head_count, HEAD), jnp.float32),
        jnp.zeros((head_count, HEAD, HEAD), jnp.float32),
    )
    shard_decay = pieces[2][-1]
    entry_pair = carried_in((shard_decay, pieces[3][-1]), "ctx", chain_link, identity)
    state_in = entry_pair[1]
    mixed, _ = finish(pieces, state_in)
    mixed_flat = mixed.reshape(row_count, local_width)
    gated_low = head_norm(mixed_flat, pre_outgate, group_gain, head_count).astype(jnp.bfloat16)
    mix_partial = jnp.dot(gated_low, out_full, preferred_element_type=jnp.float32)
    resid = inputs + lax.psum(mix_partial, "tp")
    second_low = rms_norm(resid, second_gain).astype(jnp.bfloat16)
    ffn_full, down_full = (
        lax.all_gather(ffn_local, "dp", axis=0, tiled=True),
        lax.all_gather(ffn_down, "dp", axis=1, tiled=True),
    )
    gate_up = jnp.dot(second_low, ffn_full, preferred_element_type=jnp.float32)
    pre_gate = gate_up[:, :hidden_width]
    pre_up = gate_up[:, hidden_width:]
    hidden_low = (jax.nn.silu(pre_gate) * pre_up).astype(jnp.bfloat16)
    ffn_partial = jnp.dot(hidden_low, down_full, preferred_element_type=jnp.float32)
    block_out = (
        resid + lax.psum(ffn_partial.astype(jnp.bfloat16), "tp").astype(jnp.float32)
    ).astype(jnp.bfloat16)
    mix_full, out_full, ffn_full, down_full = (
        lax.all_gather(mix_local, "dp", axis=0, tiled=True),
        lax.all_gather(out_proj, "dp", axis=1, tiled=True),
        lax.all_gather(ffn_local, "dp", axis=0, tiled=True),
        lax.all_gather(ffn_down, "dp", axis=1, tiled=True),
    )
    cotangent_full = cotangent.astype(jnp.float32)
    hidden_grad = contract_last(cotangent, down_full)
    down_weight_grad = contract_first(hidden_low, cotangent)
    _, act_pull = jax.vjp(lambda gate_in, up_in: jax.nn.silu(gate_in) * up_in, pre_gate, pre_up)
    gate_grad, up_grad = act_pull(hidden_grad)
    gate_up_grad = jnp.concatenate([gate_grad, up_grad], axis=1).astype(jnp.bfloat16)
    second_part = contract_last(gate_up_grad, ffn_full)
    ffn_weight_grad = contract_first(second_low, gate_up_grad)
    second_total = lax.psum(second_part, "tp")
    _, second_pull = jax.vjp(rms_norm, resid, second_gain)
    resid_part, second_gain_grad = second_pull(second_total)
    resid_grad = cotangent_full + resid_part
    resid_low = resid_grad.astype(jnp.bfloat16)
    gated_grad = contract_last(resid_low, out_full)
    out_weight_grad = contract_first(gated_low, resid_low)
    _, head_pull = jax.vjp(
        lambda mixed_in, gate_in, gain_in: head_norm(mixed_in, gate_in, gain_in, head_count),
        mixed_flat,
        pre_outgate,
        group_gain,
    )
    mixed_grad, outgate_pre_grad, group_gain_grad = head_pull(gated_grad)
    _, mixer_pull = jax.vjp(
        mixer,
        to_heads(queries),
        to_heads(key_rows),
        to_heads(pre_value),
        to_heads(log_forget),
        state_in,
    )
    first_pass = mixer_pull(
        (to_heads(mixed_grad), jnp.zeros((head_count, HEAD, HEAD), jnp.float32))
    )
    after_pair = carried_in_2((shard_decay, first_pass[4]), "ctx", chain_link, identity)
    second_pass = mixer_pull((jnp.zeros((row_count, head_count, HEAD), jnp.float32), after_pair[1]))
    query_rec_grad = (first_pass[0] + second_pass[0]).reshape(row_count, local_width)
    key_rec_grad = (first_pass[1] + second_pass[1]).reshape(row_count, local_width)
    value_rec_grad = (first_pass[2] + second_pass[2]).reshape(row_count, local_width)
    log_rec_grad = (first_pass[3] + second_pass[3]).reshape(row_count, local_width)
    _, gate_pull = jax.vjp(gate_values, pre_query, pre_forget, forget_bias, bound_vec)
    query_pre_grad, forget_pre_grad, forget_bias_grad, bound_grad = gate_pull(
        (query_rec_grad, key_rec_grad, log_rec_grad)
    )
    _, table_pull = jax.vjp(lambda rows_in: lower_bound(rows_in, layer_index), bound_table)
    (table_grad,) = table_pull(bound_grad)
    proj_grad = jnp.concatenate(
        [query_pre_grad, forget_pre_grad, value_rec_grad, outgate_pre_grad], axis=1
    ).astype(jnp.bfloat16)
    first_part = contract_last(proj_grad, mix_full)
    mix_weight_grad = contract_first(first_low, proj_grad)
    first_total = lax.psum(first_part.astype(jnp.bfloat16), "tp").astype(jnp.float32)
    _, first_pull = jax.vjp(rms_norm, inputs, first_gain)
    input_part, first_gain_grad = first_pull(first_total)
    input_grad = resid_grad + input_part
    mix_summed, out_summed, ffn_summed, down_summed = (
        lax.psum_scatter(
            mix_weight_grad.astype(jnp.bfloat16), ("dp", "ctx"), scatter_dimension=0, tiled=True
        ).astype(jnp.float32),
        lax.psum_scatter(
            out_weight_grad.astype(jnp.bfloat16), ("dp", "ctx"), scatter_dimension=1, tiled=True
        ).astype(jnp.float32),
        lax.psum_scatter(
            ffn_weight_grad.astype(jnp.bfloat16), ("dp", "ctx"), scatter_dimension=0, tiled=True
        ).astype(jnp.float32),
        lax.psum_scatter(
            down_weight_grad.astype(jnp.bfloat16), ("dp", "ctx"), scatter_dimension=1, tiled=True
        ).astype(jnp.float32),
    )
    mix_shard, out_shard, ffn_shard, down_shard = (
        lax.all_gather(mix_summed.astype(jnp.bfloat16), "ctx", axis=0, tiled=True).astype(
            mix_summed.dtype
        ),
        lax.all_gather(out_summed.astype(jnp.bfloat16), "ctx", axis=1, tiled=True).astype(
            out_summed.dtype
        ),
        lax.all_gather(ffn_summed.astype(jnp.bfloat16), "ctx", axis=0, tiled=True).astype(
            ffn_summed.dtype
        ),
        lax.all_gather(down_summed.astype(jnp.bfloat16), "ctx", axis=1, tiled=True).astype(
            down_summed.dtype
        ),
    )
    first_sum, second_sum, group_sum, bias_sum, table_sum = (
        lax.psum(first_gain_grad.astype(jnp.bfloat16), ("dp", "ctx")).astype(jnp.float32),
        lax.psum(second_gain_grad.astype(jnp.bfloat16), ("dp", "ctx")).astype(jnp.float32),
        lax.psum(group_gain_grad.astype(jnp.bfloat16), ("dp", "ctx")).astype(jnp.float32),
        lax.psum(forget_bias_grad.astype(jnp.bfloat16), ("dp", "ctx")).astype(jnp.float32),
        lax.psum(table_grad.astype(jnp.bfloat16), ("dp", "ctx")).astype(jnp.float32),
    )
    return (
        block_out,
        input_grad,
        mix_shard[:, :local_width],
        mix_shard[:, local_width : 2 * local_width],
        mix_shard[:, 2 * local_width : 3 * local_width],
        mix_shard[:, 3 * local_width :],
        out_shard,
        ffn_shard[:, :hidden_width],
        ffn_shard[:, hidden_width:],
        down_shard,
        first_sum,
        second_sum,
        group_sum,
        bias_sum,
        table_sum,
    )


def solution(mesh):
    return jax.shard_map(
        body,
        mesh=mesh,
        in_specs=(
            P(("dp", "ctx"), None),
            P("dp", "tp"),
            P("dp", "tp"),
            P("dp", "tp"),
            P("dp", "tp"),
            P("tp", "dp"),
            P("dp", "tp"),
            P("dp", "tp"),
            P("tp", "dp"),
            P(),
            P(),
            P("tp"),
            P("tp"),
            P(None, "tp"),
            P(),
            P("dp"),
            P(("dp", "ctx"), None),
        ),
        out_specs=(
            P(("dp", "ctx"), None),
            P(("dp", "ctx"), None),
            P("dp", "tp"),
            P("dp", "tp"),
            P("dp", "tp"),
            P("dp", "tp"),
            P("tp", "dp"),
            P("dp", "tp"),
            P("dp", "tp"),
            P("tp", "dp"),
            P(),
            P(),
            P("tp"),
            P("tp"),
            P(None, "tp"),
        ),
        check_vma=False,
    )
```

profile of v0, /device:TPU:0, one launch (start us, length us, event | category | flops | bytes accessed | tf_op | source)
XLA Modules:
  0.0 2218.8 jit_solution(17821822070272523341)
XLA Ops:
  17.0 145.9 %all-gather.8.cloned.1.call-done = bf16[2048,2048]{1,0:T(8,128)(2,1)} async-done(((bf16[512,2048]{1,0:T(8,128)(2,1)}), bf16[2048,2048]{1,0:T(8,128)(2,1)}) %all-gather.8.cloned.1.call-update) | async-done | bytes 8388624 | tf_op jit(solution)/shard_map/all_gather | solution.py:170
  162.8 12.6 fusion.115
  209.9 13.7 fusion.85
  268.4 18.6 pad.557
  287.0 12.1 pad.558
  312.1 35.5 %pad.734 = f32[31,4,128,128]{2,3,1,0:T(8,128)} pad(f32[16,4,128,128]{2,3,1,0:T(8,128)} %pad_maximum_fusion.5, f32[]{:T(128)} %constant.113.clone.1), padding=0_0_1x0_0_0x0_0_0x0_0_0 | pad | bytes 12320772 | tf_op jit(solution)/shard_map/slice | solution.py:135
  347.6 35.6 %pad.559 = f32[32,4,128,128]{2,3,1,0:T(8,128)} pad(f32[16,4,128,128]{2,3,1,0:T(8,128)} %pad_maximum_fusion.5, f32[]{:T(128)} %constant.113.clone.1), padding=0_1_1x0_0_0x0_0_0x0_0_0 | pad | bytes 12582916 | tf_op jit(solution)/shard_map/pad | solution.py:128
  385.0 35.6 %pad.1005 = f32[32,4,128,128]{2,3,1,0:T(8,128)} pad(f32[16,4,128,128]{2,3,1,0:T(8,128)} %add.591, f32[]{:T(128)} %constant.113.clone.1), padding=1_0_1x0_0_0x0_0_0x0_0_0 | pad | bytes 12582916
  438.1 12.0 multiply_add_fusion
  450.2 16.1 fusion.19
  499.8 166.2 %all-reduce.122.cloned.1.call-done = f32[1024,2048]{1,0:T(8,128)} async-done(((f32[1024,2048]{1,0:T(8,128)}), f32[1024,2048]{1,0:T(8,128)}) %all-reduce.122.cloned.1.call-update) | async-done | bytes 8388624 | tf_op jit(solution)/shard_map/psum | solution.py:212
  675.0 194.9 %all-gather.12.cloned.1.call-done = bf16[2048,2816]{1,0:T(8,128)(2,1)} async-done(((bf16[512,2816]{1,0:T(8,128)(2,1)}), bf16[2048,2816]{1,0:T(8,128)(2,1)}) %all-gather.12.cloned.1.call-update) | async-done | bytes 11534352 | tf_op jit(solution)/shard_map/all_gather | solution.py:215
  869.9 20.0 fusion.177
  889.9 86.4 %all-gather.14.cloned.1.call-done = bf16[1408,2048]{1,0:T(8,128)(2,1)} async-done(((bf16[1408,512]{1,0:T(8,128)(2,1)}), bf16[1408,2048]{1,0:T(8,128)(2,1)}) %all-gather.14.cloned.1.call-update) | async-done | bytes 5767184 | tf_op jit(solution)/shard_map/all_gather | solution.py:216
  976.3 16.2 fusion.15
  995.1 16.8 fusion.20
  1012.0 10.5 convolution_convert_fusion.1
  1024.9 11.3 fusion.17
  1054.8 18.7 convolution_convert_fusion
  1073.5 11.1 convolution_convert_fusion.4
  1084.6 97.8 %all-reduce.124.cloned.1.call-done = f32[1024,2048]{1,0:T(8,128)} async-done(((f32[1024,2048]{1,0:T(8,128)}), f32[1024,2048]{1,0:T(8,128)}) %all-reduce.124.cloned.1.call-update) | async-done | bytes 8388624 | tf_op jit(solution)/shard_map/psum | solution.py:240
  1214.6 13.5 fusion.78
  1364.9 10.2 pad.622
  1401.0 12.0 pad.589
  1413.1 18.5 pad.623
  1435.8 18.6 pad.624
  1454.4 12.1 pad.590
  1466.5 16.7 pad.568
  1483.2 10.8 pad.602
  1494.0 15.5 multiply_reduce_fusion.5
  1510.5 35.6 %pad.625 = f32[32,4,128,128]{2,3,1,0:T(8,128)} pad(f32[16,4,128,128]{2,3,1,0:T(8,128)} %get-tuple-element.256, f32[]{:T(128)} %constant.113.clone.1), padding=1_0_1x0_0_0x0_0_0x0_0_0 | pad | bytes 12582916 | tf_op jit(solution)/shard_map/transpose(jvp())/pad | solution.py:128
  1546.0 35.5 %pad.591 = f32[32,4,128,128]{2,3,1,0:T(8,128)} pad(f32[16,4,128,128]{2,3,1,0:T(8,128)} %get-tuple-element.255, f32[]{:T(128)} %constant.113.clone.1), padding=1_0_1x0_0_0x0_0_0x0_0_0 | pad | bytes 12582916 | tf_op jit(solution)/shard_map/transpose(jvp())/pad | solution.py:128
  1590.3 35.6 %pad.592 = f32[32,4,128,128]{2,3,1,0:T(8,128)} pad(f32[16,4,128,128]{2,3,1,0:T(8,128)} %get-tuple-element.375, f32[]{:T(128)} %constant.113.clone.1), padding=0_1_1x0_0_0x0_0_0x0_0_0 | pad | bytes 12582916 | tf_op jit(solution)/shard_map/transpose(jvp())/pad | solution.py:128
  1625.9 35.7 %pad.626 = f32[32,4,128,128]{2,3,1,0:T(8,128)} pad(f32[16,4,128,128]{2,3,1,0:T(8,128)} %get-tuple-element.376, f32[]{:T(128)} %constant.113.clone.1), padding=0_1_1x0_0_0x0_0_0x0_0_0 | pad | bytes 12582916 | tf_op jit(solution)/shard_map/transpose(jvp())/pad | solution.py:128
  1661.7 33.6 %pad.562 = f32[32,4,128,128]{2,3,1,0:T(8,128)} pad(f32[15,4,128,128]{2,3,1,0:T(8,128)} %get-tuple-element.290, f32[]{:T(128)} %constant.113.clone.1), padding=2_1_1x0_0_0x0_0_0x0_0_0 | pad | bytes 12320772 | tf_op jit(solution)/shard_map/transpose(jvp())/pad | solution.py:128
  1695.3 33.7 %pad.597 = f32[32,4,128,128]{2,3,1,0:T(8,128)} pad(f32[15,4,128,128]{2,3,1,0:T(8,128)} %get-tuple-element.291, f32[]{:T(128)} %constant.113.clone.1), padding=2_1_1x0_0_0x0_0_0x0_0_0 | pad | bytes 12320772 | tf_op jit(solution)/shard_map/transpose(jvp())/pad | solution.py:128
  1729.0 10.8 fusion.18
  1752.8 10.0 add_add_fusion.3
  1771.4 15.1 fusion.83
  1786.5 9.8 add_add_fusion.2
  1810.3 19.3 fusion.176
  1830.9 11.6 fusion.41
  1842.6 13.5 fusion.81
  1877.1 12.9 convolution_convert_fusion.3
  1890.7 14.5 convolution_convert_fusion.2
  1913.4 152.0 %all-reduce.126.cloned.1.call-done = (bf16[1024,2048]{1,0:T(8,128)(2,1)}, bf16[1024,2048]{1,0:T(8,128)(2,1)}) async-done(((bf16[1024,2048]{1,0:T(8,128)(2,1)}, bf16[1024,2048]{1,0:T(8,128)(2,1)}), (bf16[1024,2048]{1,0:T(8,128)(2,1)}, bf16[1024,2048]{1,0:T(8,128)(2,1)})) %all-reduce.126.cloned.1.call-update) | async-done | bytes 8388624 | tf_op jit(solution)/shard_map/psum | solution.py:224
  2073.8 84.8 %reduce-scatter.5.cloned.1.call-done = bf16[256,2048]{1,0:T(8,128)(2,1)} async-done(((bf16[2048,2048]{1,0:T(8,128)(2,1)}), bf16[256,2048]{1,0:T(8,128)(2,1)}) %reduce-scatter.5.cloned.1.call-update) | async-done | bytes 1048592 | tf_op jit(solution)/shard_map/reduce_scatter | solution.py:287
  2164.6 26.3 %all-reduce.116 = (bf16[2048]{0:T(1024)(128)(2,1)S(1)}, bf16[2048]{0:T(1024)(128)(2,1)S(1)}, bf16[512]{0:T(512)(128)(2,1)S(1)}, bf16[512]{0:T(512)(128)(2,1)S(1)}, bf16[24,512]{1,0:T(8,128)(2,1)S(1)}) all-reduce(bf16[2048]{0:T(1024)(128)(2,1)S(1)} %get-tuple-element.200, ...), channel_id=1, replica_groups=mesh['dp'=4,'ctx'=2,'tp'=4] {'dp','ctx'}, use_global_device_ids=true, to_apply=%region_51.52 | all-reduce | flops 17408 | bytes 69632 | tf_op jit(solution)/shard_map/psum | solution.py:315
  (808 shorter events, 494.5 us)
Async XLA Ops:
  7.2 155.7 %all-gather.8.cloned.1.call-start = ((), (), s32[]{:S(2)}) async-start(), calls=%async_computation.4 | async-start | bytes 10485760 | tf_op jit(solution)/shard_map/all_gather | solution.py:170
  10.4 477.5 %all-gather.10.cloned.1.call-start = ((), (), s32[]{:S(2)}) async-start(), calls=%async_computation.5 | async-start | bytes 2621440 | tf_op jit(solution)/shard_map/all_gather | solution.py:171
  11.1 654.9 %all-reduce.122.cloned.1.call-start = ((), (), s32[]{:S(2)}) async-start(), calls=%async_computation.6 | async-start | bytes 16777216 | tf_op jit(solution)/shard_map/psum | solution.py:212
  12.7 150.1 %copy-start.194 = (f32[2048]{0:T(1024)S(1)}, f32[2048]{0:T(1024)}, u32[]{:S(2)}) copy-start(f32[2048]{0:T(1024)} %param.28) | copy-start | bytes 24580
  16.4 159.0 %copy-start.171 = (f32[1024]{0:T(1024)}, f32[1024]{0:T(1024)S(1)}, u32[]{:S(2)}) copy-start(f32[1024]{0:T(1024)S(1)} %fusion.149) | copy-start | bytes 12292
  16.6 158.8 %copy-start.178 = (f32[512]{0:T(512)}, f32[512]{0:T(512)S(1)}, u32[]{:S(2)}) copy-start(f32[512]{0:T(512)S(1)} %multiply_reduce_fusion.28) | copy-start | bytes 6148
  16.6 158.8 %copy-start.196 = (f32[512]{0:T(512)}, f32[512]{0:T(512)S(1)}, u32[]{:S(2)}) copy-start(f32[512]{0:T(512)S(1)} %broadcast_subtract_fusion) | copy-start | bytes 6148
  16.7 169.4 %copy-start.214 = (f32[32]{0:T(128)}, f32[32]{0:T(128)S(1)}, u32[]{:S(2)}) copy-start(f32[32]{0:T(128)S(1)} %get-tuple-element.269) | copy-start | bytes 388
  16.9 1024.1 %copy-start.73 = (pred[32,32,32]{2,1,0:T(8,128)(4,1)}, pred[32,32,32]{2,1,0:T(8,128)(4,1)S(1)}, u32[]{:S(2)}) copy-start(pred[32,32,32]{2,1,0:T(8,128)(4,1)S(1)} %compare_and_fusion) | copy-start | bytes 98308
  16.9 189.3 %copy-start.131 = (f32[32,32]{0,1:T(8,128)}, f32[32,32]{0,1:T(8,128)S(1)}, u32[]{:S(2)}) copy-start(f32[32,32]{0,1:T(8,128)S(1)} %get-tuple-element.440) | copy-start | bytes 12292
  16.9 415.8 %copy-start.129 = (f32[32,32]{0,1:T(8,128)}, f32[32,32]{0,1:T(8,128)S(1)}, u32[]{:S(2)}) copy-start(f32[32,32]{0,1:T(8,128)S(1)} %get-tuple-element.439) | copy-start | bytes 12292
  17.0 158.5 %copy-start.204 = (f32[512]{0:T(512)S(1)}, f32[512]{0:T(512)}, u32[]{:S(2)}) copy-start(f32[512]{0:T(512)} %param.31) | copy-start | bytes 6148
  184.2 22.0 copy-start
  187.5 36.2 %copy-start.125 = (f32[16,4,128]{2,1,0:T(4,128)}, f32[16,4,128]{2,1,0:T(4,128)S(1)}, u32[]{:S(2)}) copy-start(f32[16,4,128]{2,1,0:T(4,128)S(1)} %get-tuple-element.356) | copy-start | bytes 98308
  187.5 39.7 %copy-start.142 = (f32[8,4,128]{2,1,0:T(4,128)}, f32[8,4,128]{2,1,0:T(4,128)S(1)}, u32[]{:S(2)}) copy-start(f32[8,4,128]{2,1,0:T(4,128)S(1)} %get-tuple-element.380) | copy-start | bytes 49156
  187.6 42.5 %copy-start.155 = (f32[4,4,128]{2,1,0:T(4,128)}, f32[4,4,128]{2,1,0:T(4,128)S(1)}, u32[]{:S(2)}) copy-start(f32[4,4,128]{2,1,0:T(4,128)S(1)} %get-tuple-element.402) | copy-start | bytes 24580
  187.6 42.6 %copy-start.165 = (f32[2,4,128]{2,1,0:T(4,128)}, f32[2,4,128]{2,1,0:T(4,128)S(1)}, u32[]{:S(2)}) copy-start(f32[2,4,128]{2,1,0:T(4,128)S(1)} %get-tuple-element.421) | copy-start | bytes 12292
  187.7 42.6 %copy-start.198 = (f32[4,128]{1,0:T(4,128)}, f32[4,128]{1,0:T(4,128)S(1)}, u32[]{:S(2)}) copy-start(f32[4,128]{1,0:T(4,128)S(1)} %get-tuple-element.431) | copy-start | bytes 6148
  347.6 35.6 %copy-start.206 = (f32[1,4,128]{2,1,0:T(4,128)S(1)}, f32[1,4,128]{2,1,0:T(4,128)}, u32[]{:S(2)}) copy-start(f32[1,4,128]{2,1,0:T(4,128)} %get-tuple-element.266) | copy-start | bytes 6148
  424.2 600.7 %copy-start.88 = (f32[1,4,128,128]{2,3,1,0:T(8,128)}, f32[1,4,128,128]{2,3,1,0:T(8,128)S(1)}, u32[]{:S(2)}) copy-start(f32[1,4,128,128]{2,3,1,0:T(8,128)S(1)} %add_select_fusion) | copy-start | bytes 786436
  495.5 374.3 %all-gather.12.cloned.1.call-start = ((), (), s32[]{:S(2)}) async-start(), calls=%async_computation.7 | async-start | bytes 14417920 | tf_op jit(solution)/shard_map/all_gather | solution.py:215
  499.2 477.1 %all-gather.14.cloned.1.call-start = ((), (), s32[]{:S(2)}) async-start(), calls=%async_computation.8 | async-start | bytes 7208960 | tf_op jit(solution)/shard_map/all_gather | solution.py:216
  499.7 370.1 %copy-start.177 = (f32[2048]{0:T(1024)S(1)}, f32[2048]{0:T(1024)}, u32[]{:S(2)}) copy-start(f32[2048]{0:T(1024)} %param.29) | copy-start | bytes 24580
  499.8 682.7 %all-reduce.124.cloned.1.call-start = ((), (), s32[]{:S(2)}) async-start(), calls=%async_computation.9 | async-start | bytes 16777216 | tf_op jit(solution)/shard_map/psum | solution.py:240
  1011.9 865.1 %reduce-scatter.11.cloned.1.call-start = ((), (), s32[]{:S(2)}) async-start(), calls=%async_computation.15 | async-start | bytes 6488064 | tf_op jit(solution)/shard_map/reduce_scatter | solution.py:296
  1022.5 882.9 %reduce-scatter.9.cloned.1.call-start = ((), (), s32[]{:S(2)}) async-start(), calls=%async_computation.13 | async-start | bytes 12976128 | tf_op jit(solution)/shard_map/reduce_scatter | solution.py:293
  1073.5 833.1 %reduce-scatter.7.cloned.1.call-start = ((), (), s32[]{:S(2)}) async-start(), calls=%async_computation.12 | async-start | bytes 2359296 | tf_op jit(solution)/shard_map/reduce_scatter | solution.py:290
  1265.8 31.7 %copy-start.157 = (f32[8,4,128]{2,1,0:T(4,128)}, f32[8,4,128]{2,1,0:T(4,128)S(1)}, u32[]{:S(2)}) copy-start(f32[8,4,128]{2,1,0:T(4,128)S(1)} %slice.479) | copy-start | bytes 49156
  1265.9 31.7 %copy-start.158 = (f32[8,4,128]{2,1,0:T(4,128)}, f32[8,4,128]{2,1,0:T(4,128)S(1)}, u32[]{:S(2)}) copy-start(f32[8,4,128]{2,1,0:T(4,128)S(1)} %slice.471) | copy-start | bytes 49156
  1546.0 35.5 %copy-start.126 = (f32[16,4,128]{2,1,0:T(4,128)S(1)}, f32[16,4,128]{2,1,0:T(4,128)}, u32[]{:S(2)}) copy-start(f32[16,4,128]{2,1,0:T(4,128)} %copy-done.125) | copy-start | bytes 98308
  1695.3 33.7 %copy-start.24 = (f32[32,4,128,32]{2,3,1,0:T(8,128)S(1)}, f32[32,4,128,32]{2,3,1,0:T(8,128)}, u32[]{:S(2)}) copy-start(f32[32,4,128,32]{2,3,1,0:T(8,128)} %copy-done.23) | copy-start | bytes 6291460
  1695.3 33.7 %copy-start.89 = (f32[1,4,128,128]{2,3,1,0:T(8,128)S(1)}, f32[1,4,128,128]{2,3,1,0:T(8,128)}, u32[]{:S(2)}) copy-start(f32[1,4,128,128]{2,3,1,0:T(8,128)} %copy-done.88) | copy-start | bytes 786436
  1771.4 33.5 %slice-start.1 = ((s8[8388608]{0:T(1024)(128)(4,1)}), s8[4194304]{0:T(1024)(128)(4,1)S(1)}, s32[]{:S(2)}) async-start(s8[8388608]{0:T(1024)(128)(4,1)} %bitcast.242), calls=%async_computation.19 | async-start | bytes 8388608
  1808.7 20.9 copy-start.134
  1808.7 20.9 copy-start.135
  1808.7 20.9 slice-start.17
  1808.7 20.9 slice-start.18
  1808.8 20.9 copy-start.215
  1808.8 101.3 %all-gather.20.cloned.1.call-start = ((), (), s32[]{:S(2)}) async-start(), calls=%async_computation.16 | async-start | bytes 2162688 | tf_op jit(solution)/shard_map/all_gather | solution.py:310
  1810.3 20.6 copy-start.48
  1810.3 20.6 copy-start.49
  1810.3 20.6 copy-start.54
  1810.3 20.6 copy-start.55
  1877.1 188.4 %all-reduce.126.cloned.1.call-start = ((), (), s32[]{:S(2)}) async-start(), calls=%async_computation.17 | async-start | bytes 16777216 | tf_op jit(solution)/shard_map/psum | solution.py:224
  1890.0 268.6 %reduce-scatter.5.cloned.1.call-start = ((), (), s32[]{:S(2)}) async-start(), calls=%async_computation.10 | async-start | bytes 9437184 | tf_op jit(solution)/shard_map/reduce_scatter | solution.py:287
  1905.3 298.1 %all-gather.18.cloned.1.call-start = ((), (), s32[]{:S(2)}) async-start(), calls=%async_computation.14 | async-start | bytes 4325376 | tf_op jit(solution)/shard_map/all_gather | solution.py:307
  1906.0 302.0 %all-gather.16.cloned.1.call-start = ((), (), s32[]{:S(2)}) async-start(), calls=%async_computation.11 | async-start | bytes 3145728 | tf_op jit(solution)/shard_map/all_gather | solution.py:301
  2158.6 35.2 %copy-start.168 = (f32[1024]{0:T(1024)S(1)}, f32[1024]{0:T(1024)}, u32[]{:S(2)}) copy-start(f32[1024]{0:T(1024)} %copy-done.167) | copy-start | bytes 12292
  (213 other events, 1256.3 us)
Sparse Core Ops, SparseCore 0:
  10.5 152.3 all-gather.7
  164.4 44.1 all-gather.9
  495.6 170.3 all-reduce.121
  668.1 201.7 all-gather.11
  871.3 104.8 all-gather.13
  1012.0 170.3 all-reduce.123
  1184.7 65.5 reduce-scatter.10
  1252.6 117.6 reduce-scatter.8
  1808.8 36.2 reduce-scatter.6
  1877.2 10.0 all-gather.19
  1891.6 173.7 all-reduce.125
  2068.3 90.2 reduce-scatter.4
  2160.2 10.1 all-gather.17
  2171.8 11.7 all-gather.15
where the time goes:
time: 2250 us; the launch traced here: 2220 us
  waiting for transfers between devices  930 us (41%)
  local copies, waits for them, and re-layouts  640 us (28%)
  matrix products  319 us (14%)
  other arithmetic  275 us (12%)
  blocking collectives  36.4 us (2%)
    pad x74, local copies, waits for them, and re-layouts, block_parts(): lax.associative_scan(chain_link, (carried, states), axis=0)  483 us
    all_gather x1, waiting for transfers between devices, body(): lax.all_gather(ffn_local, 'dp', axis=0, tiled=True)  195 us
    psum x1, waiting for transfers between devices, body(): resid = inputs + lax.psum(mix_partial, 'tp')  166 us
    psum x1, waiting for transfers between devices, body(): lax.psum(ffn_partial.astype(jnp.bfloat16), 'tp').astype(jnp.float32)  152 us
    all_gather x1, waiting for transfers between devices, body(): lax.all_gather(mix_local, 'dp', axis=0, tiled=True)  146 us
    psum x1, waiting for transfers between devices, body(): second_total = lax.psum(second_part, 'tp')  97.8 us
    all_gather x1, waiting for transfers between devices, body(): lax.all_gather(ffn_down, 'dp', axis=1, tiled=True)  86.4 us
    reduce_scatter x1, waiting for transfers between devices, body(): lax.psum_scatter(mix_weight_grad.astype(jnp.bfloat16), ('dp', 'ctx'), sca...  84.8 us
  transfers between devices with their start and end apart: 14, of which 7 were waited for; matrix products, arithmetic and copies ran while one was open for 51% of the time, Pallas kernels for 0%

commit v1 on v0

--- a/solution.py
+++ b/solution.py
@@ -237,7 +237,11 @@
     gate_up_grad = jnp.concatenate([gate_grad, up_grad], axis=1).astype(jnp.bfloat16)
     second_part = contract_last(gate_up_grad, ffn_full)
     ffn_weight_grad = contract_first(second_low, gate_up_grad)
-    second_total = lax.psum(second_part, "tp")
+    second_total = second_part
+    for hop_ in (1, 2):
+        second_total = second_total + lax.ppermute(
+            second_total, "tp", [(dev, dev ^ hop_) for dev in range(4)]
+        )
     _, second_pull = jax.vjp(rms_norm, resid, second_gain)
     resid_part, second_gain_grad = second_pull(second_total)
     resid_grad = cotangent_full + resid_part

time: 2250 us -> 2470 us (1.098)
  waiting for transfers between devices: 930 us -> 1150 us
  local copies, waits for them, and re-layouts: 640 us -> 602 us
    ppermute x0 -> x2, waiting for transfers between devices: none -> 322 us  [body(): lax.ppermute(second_total, 'tp', [(dev, dev ^ hop_) for dev in range(4)])]
    psum x1 -> x0, waiting for transfers between devices: 97.8 us -> none  [body(): second_total = lax.psum(second_part, 'tp')]
    pad x74, local copies, waits for them, and re-layouts: 483 us -> 456 us  [block_parts(): lax.associative_scan(chain_link, (carried, states), axis=0)]
    unnamed x468 -> x426, local copies, waits for them, and re-layouts: 79.2 us -> 67.2 us
  transfers between devices with their start and end apart: 14 -> 15, of which waited for: 7 -> 8; matrix products, arithmetic and copies ran while one was open for 51% -> 47% of each run, Pallas kernels for 0% -> 0%
where the time goes in v1:
time: 2470 us; the launch traced here: 2430 us
  waiting for transfers between devices  1150 us (47%)
  local copies, waits for them, and re-layouts  602 us (24%)
  matrix products  323 us (13%)
  other arithmetic  297 us (12%)
  blocking collectives  36.4 us (1%)
    pad x74, local copies, waits for them, and re-layouts, block_parts(): lax.associative_scan(chain_link, (carried, states), axis=0)  456 us
    ppermute x2, waiting for transfers between devices, body(): lax.ppermute(second_total, 'tp', [(dev, dev ^ hop_) for dev in range(4)])  322 us
    all_gather x1, waiting for transfers between devices, body(): lax.all_gather(ffn_local, 'dp', axis=0, tiled=True)  195 us
    psum x1, waiting for transfers between devices, body(): resid = inputs + lax.psum(mix_partial, 'tp')  166 us
    psum x1, waiting for transfers between devices, body(): lax.psum(ffn_partial.astype(jnp.bfloat16), 'tp').astype(jnp.float32)  148 us
    all_gather x1, waiting for transfers between devices, body(): lax.all_gather(mix_local, 'dp', axis=0, tiled=True)  146 us
    all_gather x1, waiting for transfers between devices, body(): lax.all_gather(ffn_down, 'dp', axis=1, tiled=True)  86.4 us
    reduce_scatter x1, waiting for transfers between devices, body(): lax.psum_scatter(mix_weight_grad.astype(jnp.bfloat16), ('dp', 'ctx'), sca...  84.9 us
  transfers between devices with their start and end apart: 15, of which 8 were waited for; matrix products, arithmetic and copies ran while one was open for 47% of the time, Pallas kernels for 0%

profile of v1, /device:TPU:0, one launch (start us, length us, event | category | flops | bytes accessed | tf_op | source)
XLA Modules:
  0.0 2430.6 jit_solution(1689016389080359105)
XLA Ops:
  17.0 145.9 %all-gather.8.cloned.1.call-done = bf16[2048,2048]{1,0:T(8,128)(2,1)} async-done(((bf16[512,2048]{1,0:T(8,128)(2,1)}), bf16[2048,2048]{1,0:T(8,128)(2,1)}) %all-gather.8.cloned.1.call-update) | async-done | bytes 8388624 | tf_op jit(solution)/shard_map/all_gather | solution.py:170
  162.8 12.6 fusion.115
  209.9 13.5 fusion.85
  268.2 18.6 pad.557
  286.8 12.1 pad.558
  311.9 35.5 %pad.734 = f32[31,4,128,128]{2,3,1,0:T(8,128)} pad(f32[16,4,128,128]{2,3,1,0:T(8,128)} %pad_maximum_fusion.5, f32[]{:T(128)} %constant.113.clone.1), padding=0_0_1x0_0_0x0_0_0x0_0_0 | pad | bytes 12320772 | tf_op jit(solution)/shard_map/slice | solution.py:135
  347.5 35.8 %pad.559 = f32[32,4,128,128]{2,3,1,0:T(8,128)} pad(f32[16,4,128,128]{2,3,1,0:T(8,128)} %pad_maximum_fusion.5, f32[]{:T(128)} %constant.113.clone.1), padding=0_1_1x0_0_0x0_0_0x0_0_0 | pad | bytes 12582916 | tf_op jit(solution)/shard_map/pad | solution.py:128
  385.0 35.8 %pad.1005 = f32[32,4,128,128]{2,3,1,0:T(8,128)} pad(f32[16,4,128,128]{2,3,1,0:T(8,128)} %add.595, f32[]{:T(128)} %constant.113.clone.1), padding=1_0_1x0_0_0x0_0_0x0_0_0 | pad | bytes 12582916
  438.5 11.7 multiply_add_fusion
  450.2 15.9 fusion.19
  499.8 166.2 %all-reduce.121.cloned.1.call-done = f32[1024,2048]{1,0:T(8,128)} async-done(((f32[1024,2048]{1,0:T(8,128)}), f32[1024,2048]{1,0:T(8,128)}) %all-reduce.121.cloned.1.call-update) | async-done | bytes 8388624 | tf_op jit(solution)/shard_map/psum | solution.py:212
  674.9 194.9 %all-gather.12.cloned.1.call-done = bf16[2048,2816]{1,0:T(8,128)(2,1)} async-done(((bf16[512,2816]{1,0:T(8,128)(2,1)}), bf16[2048,2816]{1,0:T(8,128)(2,1)}) %all-gather.12.cloned.1.call-update) | async-done | bytes 11534352 | tf_op jit(solution)/shard_map/all_gather | solution.py:215
  869.8 20.1 fusion.177
  889.9 86.4 %all-gather.14.cloned.1.call-done = bf16[1408,2048]{1,0:T(8,128)(2,1)} async-done(((bf16[1408,512]{1,0:T(8,128)(2,1)}), bf16[1408,2048]{1,0:T(8,128)(2,1)}) %all-gather.14.cloned.1.call-update) | async-done | bytes 5767184 | tf_op jit(solution)/shard_map/all_gather | solution.py:216
  976.2 16.9 fusion.15
  1002.9 19.4 convolution_convert_fusion
  1022.3 18.9 fusion.20
  1042.7 181.3 %collective-permute-done = f32[1024,2048]{1,0:T(8,128)} collective-permute-done((f32[1024,2048]{1,0:T(8,128)}, f32[1024,2048]{1,0:T(8,128)}, u32[]{:S(2)}, u32[]{:S(2)}) %collective-permute-start) | collective-permute-done | bytes 8388640 | tf_op jit(solution)/shard_map/ppermute | solution.py:242
  1223.9 11.7 add.608
  1238.9 10.9 fusion.17
  1276.8 140.7 %collective-permute-done.1 = f32[1024,2048]{1,0:T(8,128)} collective-permute-done((f32[1024,2048]{1,0:T(8,128)}, f32[1024,2048]{1,0:T(8,128)}, u32[]{:S(2)}, u32[]{:S(2)}) %collective-permute-start.1) | collective-permute-done | bytes 8388640 | tf_op jit(solution)/shard_map/ppermute | solution.py:242
  1417.6 10.5 multiply_reduce_fusion
  1455.5 11.6 fusion.18
  1480.2 13.8 fusion.78
  1586.5 10.2 pad.587
  1636.6 18.5 pad.589
  1659.2 12.1 pad.623
  1671.3 18.7 pad.624
  1690.0 12.1 pad.590
  1702.2 16.8 pad.568
  1718.9 10.9 pad.602
  1729.8 15.5 multiply_reduce_fusion.5
  1745.3 35.6 %pad.625 = f32[32,4,128,128]{2,3,1,0:T(8,128)} pad(f32[16,4,128,128]{2,3,1,0:T(8,128)} %get-tuple-element.256, f32[]{:T(128)} %constant.113.clone.1), padding=1_0_1x0_0_0x0_0_0x0_0_0 | pad | bytes 12582916 | tf_op jit(solution)/shard_map/transpose(jvp())/pad | solution.py:128
  1789.7 35.6 %pad.591 = f32[32,4,128,128]{2,3,1,0:T(8,128)} pad(f32[16,4,128,128]{2,3,1,0:T(8,128)} %get-tuple-element.255, f32[]{:T(128)} %constant.113.clone.1), padding=1_0_1x0_0_0x0_0_0x0_0_0 | pad | bytes 12582916 | tf_op jit(solution)/shard_map/transpose(jvp())/pad | solution.py:128
  1825.3 35.7 %pad.592 = f32[32,4,128,128]{2,3,1,0:T(8,128)} pad(f32[16,4,128,128]{2,3,1,0:T(8,128)} %get-tuple-element.375, f32[]{:T(128)} %constant.113.clone.1), padding=0_1_1x0_0_0x0_0_0x0_0_0 | pad | bytes 12582916 | tf_op jit(solution)/shard_map/transpose(jvp())/pad | solution.py:128
  1861.0 33.8 %pad.562 = f32[32,4,128,128]{2,3,1,0:T(8,128)} pad(f32[15,4,128,128]{2,3,1,0:T(8,128)} %get-tuple-element.290, f32[]{:T(128)} %constant.113.clone.1), padding=2_1_1x0_0_0x0_0_0x0_0_0 | pad | bytes 12320772 | tf_op jit(solution)/shard_map/transpose(jvp())/pad | solution.py:128
  1913.4 15.1 fusion.83
  1931.9 35.7 %pad.626 = f32[32,4,128,128]{2,3,1,0:T(8,128)} pad(f32[16,4,128,128]{2,3,1,0:T(8,128)} %get-tuple-element.376, f32[]{:T(128)} %constant.113.clone.1), padding=0_1_1x0_0_0x0_0_0x0_0_0 | pad | bytes 12582916 | tf_op jit(solution)/shard_map/transpose(jvp())/pad | solution.py:128
  1967.6 33.6 %pad.597 = f32[32,4,128,128]{2,3,1,0:T(8,128)} pad(f32[15,4,128,128]{2,3,1,0:T(8,128)} %get-tuple-element.291, f32[]{:T(128)} %constant.113.clone.1), padding=2_1_1x0_0_0x0_0_0x0_0_0 | pad | bytes 12320772 | tf_op jit(solution)/shard_map/transpose(jvp())/pad | solution.py:128
  2001.3 10.2 add_add_fusion.2
  2018.9 14.6 fusion.176
  2040.3 15.1 fusion.81
  2068.2 14.0 fusion.41
  2093.9 12.6 convolution_convert_fusion.3
  2107.2 14.5 convolution_convert_fusion.2
  2129.7 147.7 %all-reduce.123.cloned.1.call-done = (bf16[1024,2048]{1,0:T(8,128)(2,1)}, bf16[1024,2048]{1,0:T(8,128)(2,1)}) async-done(((bf16[1024,2048]{1,0:T(8,128)(2,1)}, bf16[1024,2048]{1,0:T(8,128)(2,1)}), (bf16[1024,2048]{1,0:T(8,128)(2,1)}, bf16[1024,2048]{1,0:T(8,128)(2,1)})) %all-reduce.123.cloned.1.call-update) | async-done | bytes 8388624 | tf_op jit(solution)/shard_map/psum | solution.py:224
  2285.7 84.9 %reduce-scatter.5.cloned.1.call-done = bf16[256,2048]{1,0:T(8,128)(2,1)} async-done(((bf16[2048,2048]{1,0:T(8,128)(2,1)}), bf16[256,2048]{1,0:T(8,128)(2,1)}) %reduce-scatter.5.cloned.1.call-update) | async-done | bytes 1048592 | tf_op jit(solution)/shard_map/reduce_scatter | solution.py:291
  2376.6 26.3 %all-reduce.116 = (bf16[2048]{0:T(1024)(128)(2,1)S(1)}, bf16[2048]{0:T(1024)(128)(2,1)S(1)}, bf16[512]{0:T(512)(128)(2,1)S(1)}, bf16[512]{0:T(512)(128)(2,1)S(1)}, bf16[24,512]{1,0:T(8,128)(2,1)S(1)}) all-reduce(bf16[2048]{0:T(1024)(128)(2,1)S(1)} %get-tuple-element.200, ...), channel_id=1, replica_groups=mesh['dp'=4,'ctx'=2,'tp'=4] {'dp','ctx'}, use_global_device_ids=true, to_apply=%region_50.51 | all-reduce | flops 17408 | bytes 69632 | tf_op jit(solution)/shard_map/psum | solution.py:319
  (763 shorter events, 492.4 us)
Async XLA Ops:
  7.2 155.7 %all-gather.8.cloned.1.call-start = ((), (), s32[]{:S(2)}) async-start(), calls=%async_computation.4 | async-start | bytes 10485760 | tf_op jit(solution)/shard_map/all_gather | solution.py:170
  10.4 477.5 %all-gather.10.cloned.1.call-start = ((), (), s32[]{:S(2)}) async-start(), calls=%async_computation.5 | async-start | bytes 2621440 | tf_op jit(solution)/shard_map/all_gather | solution.py:171
  11.1 654.8 %all-reduce.121.cloned.1.call-start = ((), (), s32[]{:S(2)}) async-start(), calls=%async_computation.6 | async-start | bytes 16777216 | tf_op jit(solution)/shard_map/psum | solution.py:212
  12.7 150.1 %copy-start.171 = (f32[2048]{0:T(1024)S(1)}, f32[2048]{0:T(1024)}, u32[]{:S(2)}) copy-start(f32[2048]{0:T(1024)} %param.28) | copy-start | bytes 24580
  16.4 159.0 %copy-start.161 = (f32[1024]{0:T(1024)}, f32[1024]{0:T(1024)S(1)}, u32[]{:S(2)}) copy-start(f32[1024]{0:T(1024)S(1)} %fusion.149) | copy-start | bytes 12292
  16.6 158.8 %copy-start.163 = (f32[512]{0:T(512)}, f32[512]{0:T(512)S(1)}, u32[]{:S(2)}) copy-start(f32[512]{0:T(512)S(1)} %multiply_reduce_fusion.28) | copy-start | bytes 6148
  16.6 158.8 %copy-start.178 = (f32[512]{0:T(512)}, f32[512]{0:T(512)S(1)}, u32[]{:S(2)}) copy-start(f32[512]{0:T(512)S(1)} %broadcast_subtract_fusion) | copy-start | bytes 6148
  16.7 169.3 %copy-start.196 = (f32[32]{0:T(128)}, f32[32]{0:T(128)S(1)}, u32[]{:S(2)}) copy-start(f32[32]{0:T(128)S(1)} %get-tuple-element.269) | copy-start | bytes 388
  16.9 1458.4 %copy-start.70 = (pred[32,32,32]{2,1,0:T(8,128)(4,1)}, pred[32,32,32]{2,1,0:T(8,128)(4,1)S(1)}, u32[]{:S(2)}) copy-start(pred[32,32,32]{2,1,0:T(8,128)(4,1)S(1)} %compare_and_fusion) | copy-start | bytes 98308
  16.9 189.2 %copy-start.126 = (f32[32,32]{0,1:T(8,128)}, f32[32,32]{0,1:T(8,128)S(1)}, u32[]{:S(2)}) copy-start(f32[32,32]{0,1:T(8,128)S(1)} %get-tuple-element.440) | copy-start | bytes 12292
  16.9 416.2 %copy-start.124 = (f32[32,32]{0,1:T(8,128)}, f32[32,32]{0,1:T(8,128)S(1)}, u32[]{:S(2)}) copy-start(f32[32,32]{0,1:T(8,128)S(1)} %get-tuple-element.439) | copy-start | bytes 12292
  17.0 158.5 %copy-start.186 = (f32[512]{0:T(512)S(1)}, f32[512]{0:T(512)}, u32[]{:S(2)}) copy-start(f32[512]{0:T(512)} %param.31) | copy-start | bytes 6148
  184.2 22.0 copy-start
  186.0 20.1 copy-start.103
  187.5 35.9 %copy-start.120 = (f32[16,4,128]{2,1,0:T(4,128)}, f32[16,4,128]{2,1,0:T(4,128)S(1)}, u32[]{:S(2)}) copy-start(f32[16,4,128]{2,1,0:T(4,128)S(1)} %get-tuple-element.356) | copy-start | bytes 98308
  187.5 39.5 %copy-start.135 = (f32[8,4,128]{2,1,0:T(4,128)}, f32[8,4,128]{2,1,0:T(4,128)S(1)}, u32[]{:S(2)}) copy-start(f32[8,4,128]{2,1,0:T(4,128)S(1)} %get-tuple-element.380) | copy-start | bytes 49156
  187.6 42.2 %copy-start.149 = (f32[4,4,128]{2,1,0:T(4,128)}, f32[4,4,128]{2,1,0:T(4,128)S(1)}, u32[]{:S(2)}) copy-start(f32[4,4,128]{2,1,0:T(4,128)S(1)} %get-tuple-element.402) | copy-start | bytes 24580
  187.6 42.3 %copy-start.156 = (f32[2,4,128]{2,1,0:T(4,128)}, f32[2,4,128]{2,1,0:T(4,128)S(1)}, u32[]{:S(2)}) copy-start(f32[2,4,128]{2,1,0:T(4,128)S(1)} %get-tuple-element.421) | copy-start | bytes 12292
  187.7 42.3 %copy-start.180 = (f32[4,128]{1,0:T(4,128)}, f32[4,128]{1,0:T(4,128)S(1)}, u32[]{:S(2)}) copy-start(f32[4,128]{1,0:T(4,128)S(1)} %get-tuple-element.431) | copy-start | bytes 6148
  268.2 18.7 copy-start.72
  347.5 35.8 %copy-start.188 = (f32[1,4,128]{2,1,0:T(4,128)S(1)}, f32[1,4,128]{2,1,0:T(4,128)}, u32[]{:S(2)}) copy-start(f32[1,4,128]{2,1,0:T(4,128)} %get-tuple-element.266) | copy-start | bytes 6148
  495.5 374.3 %all-gather.12.cloned.1.call-start = ((), (), s32[]{:S(2)}) async-start(), calls=%async_computation.7 | async-start | bytes 14417920 | tf_op jit(solution)/shard_map/all_gather | solution.py:215
  499.1 477.1 %all-gather.14.cloned.1.call-start = ((), (), s32[]{:S(2)}) async-start(), calls=%async_computation.8 | async-start | bytes 7208960 | tf_op jit(solution)/shard_map/all_gather | solution.py:216
  499.7 370.1 %copy-start.175 = (f32[2048]{0:T(1024)S(1)}, f32[2048]{0:T(1024)}, u32[]{:S(2)}) copy-start(f32[2048]{0:T(1024)} %param.29) | copy-start | bytes 24580
  499.7 777.0 %reduce-scatter.11.cloned.1.call-start = ((), (), s32[]{:S(2)}) async-start(), calls=%async_computation.14 | async-start | bytes 6488064 | tf_op jit(solution)/shard_map/reduce_scatter | solution.py:300
  976.2 18.5 copy-start.81
  1002.8 1119.0 %reduce-scatter.9.cloned.1.call-start = ((), (), s32[]{:S(2)}) async-start(), calls=%async_computation.12 | async-start | bytes 12976128 | tf_op jit(solution)/shard_map/reduce_scatter | solution.py:297
  1022.3 1100.2 %all-gather.20.cloned.1.call-start = ((), (), s32[]{:S(2)}) async-start(), calls=%async_computation.15 | async-start | bytes 2162688 | tf_op jit(solution)/shard_map/all_gather | solution.py:314
  1041.2 195.9 %copy-start.198 = (bf16[1,4,128]{2,1,0:T(4,128)(2,1)S(1)}, bf16[1,4,128]{2,1,0:T(4,128)(2,1)}, u32[]{:S(2)}) copy-start(bf16[1,4,128]{2,1,0:T(4,128)(2,1)} %get-tuple-element.265) | copy-start | bytes 3076
  1041.2 182.7 %collective-permute-start = (f32[1024,2048]{1,0:T(8,128)}, f32[1024,2048]{1,0:T(8,128)}, u32[]{:S(2)}, u32[]{:S(2)}) collective-permute-start(f32[1024,2048]{1,0:T(8,128)} %fusion.20), channel_id=1, source_target_pairs={{0,1},{1,0},{2,3},{3,2},{4,5},{5,4},{6,7},{7,6},{8,9},{9,8},{10,11... | collective-permute-start | bytes 25165832 | tf_op jit(solution)/shard_map/ppermute | solution.py:242
  1235.7 181.9 %collective-permute-start.1 = (f32[1024,2048]{1,0:T(8,128)}, f32[1024,2048]{1,0:T(8,128)}, u32[]{:S(2)}, u32[]{:S(2)}) collective-permute-start(f32[1024,2048]{1,0:T(8,128)} %add.608), channel_id=1, source_target_pairs={{0,2},{1,3},{2,0},{3,1},{4,6},{5,7},{6,4},{7,5},{8,10},{9,11},{10,... | collective-permute-start | bytes 25165832 | tf_op jit(solution)/shard_map/ppermute | solution.py:242
  1276.8 849.4 %reduce-scatter.7.cloned.1.call-start = ((), (), s32[]{:S(2)}) async-start(), calls=%async_computation.11 | async-start | bytes 2359296 | tf_op jit(solution)/shard_map/reduce_scatter | solution.py:294
  1455.5 24.7 %copy-start.25 = (f32[32,4,128,32]{2,3,1,0:T(8,128)}, f32[32,4,128,32]{2,3,1,0:T(8,128)S(1)}, u32[]{:S(2)}) copy-start(f32[32,4,128,32]{2,3,1,0:T(8,128)S(1)} %fusion.21) | copy-start | bytes 6291460
  1636.6 18.5 copy-start.136
  1671.3 18.7 copy-start.77
  1745.3 35.7 %copy-start.121 = (f32[16,4,128]{2,1,0:T(4,128)S(1)}, f32[16,4,128]{2,1,0:T(4,128)}, u32[]{:S(2)}) copy-start(f32[16,4,128]{2,1,0:T(4,128)} %copy-done.120) | copy-start | bytes 98308
  1861.0 33.8 %slice-start.6 = ((f32[16,4,128,128]{2,3,1,0:T(8,128)}), f32[1,4,128,128]{2,3,1,0:T(8,128)S(1)}, s32[]{:S(2)}) async-start(f32[16,4,128,128]{2,3,1,0:T(8,128)} %slice.453), calls=%async_computation.23 | async-start | bytes 524288 | tf_op jit(solution)/shard_map/transpose(jvp())/split | solution.py:128
  1928.7 38.9 %copy-start.137 = (f32[16,4,128]{2,1,0:T(4,128)}, f32[16,4,128]{2,1,0:T(4,128)S(1)}, u32[]{:S(2)}) copy-start(f32[16,4,128]{2,1,0:T(4,128)S(1)} %slice.469) | copy-start | bytes 98308
  1928.7 38.8 %copy-start.138 = (f32[16,4,128]{2,1,0:T(4,128)}, f32[16,4,128]{2,1,0:T(4,128)S(1)}, u32[]{:S(2)}) copy-start(f32[16,4,128]{2,1,0:T(4,128)S(1)} %slice.477) | copy-start | bytes 98308
  1967.6 33.6 %slice-start.7 = ((f32[16,4,128,128]{2,3,1,0:T(8,128)}), f32[1,4,128,128]{2,3,1,0:T(8,128)S(1)}, s32[]{:S(2)}) async-start(f32[16,4,128,128]{2,3,1,0:T(8,128)} %copy-done.61), calls=%async_computation.24 | async-start | bytes 524288 | tf_op jit(solution)/shard_map/transpose(jvp())/split | solution.py:128
  2001.2 17.5 copy-start.104
  2034.6 20.9 slice-start.1
  2037.1 18.4 slice-start.2
  2059.3 218.1 %all-reduce.123.cloned.1.call-start = ((), (), s32[]{:S(2)}) async-start(), calls=%async_computation.16 | async-start | bytes 16777216 | tf_op jit(solution)/shard_map/psum | solution.py:224
  2106.5 264.1 %reduce-scatter.5.cloned.1.call-start = ((), (), s32[]{:S(2)}) async-start(), calls=%async_computation.9 | async-start | bytes 9437184 | tf_op jit(solution)/shard_map/reduce_scatter | solution.py:291
  2121.7 293.7 %all-gather.18.cloned.1.call-start = ((), (), s32[]{:S(2)}) async-start(), calls=%async_computation.13 | async-start | bytes 4325376 | tf_op jit(solution)/shard_map/all_gather | solution.py:311
  2122.3 297.8 %all-gather.16.cloned.1.call-start = ((), (), s32[]{:S(2)}) async-start(), calls=%async_computation.10 | async-start | bytes 3145728 | tf_op jit(solution)/shard_map/all_gather | solution.py:305
  2370.6 35.2 %copy-start.158 = (f32[1024]{0:T(1024)S(1)}, f32[1024]{0:T(1024)}, u32[]{:S(2)}) copy-start(f32[1024]{0:T(1024)} %copy-done.157) | copy-start | bytes 12292
  (189 other events, 1128.4 us)
Sparse Core Ops, SparseCore 0:
  10.5 152.3 all-gather.7
  164.4 44.1 all-gather.9
  495.6 170.3 all-reduce.120
  668.0 201.7 all-gather.11
  871.3 104.8 all-gather.13
  1002.9 63.0 reduce-scatter.10
  1068.5 117.6 reduce-scatter.8
  1276.9 6.7 all-gather.19
  2059.4 33.9 reduce-scatter.6
  2106.7 170.6 all-reduce.122
  2280.3 90.2 reduce-scatter.4
  2372.0 10.0 all-gather.17
  2383.7 11.7 all-gather.15
